TPU v7x, 32 devices: a whole 2x2x4 slice. The times are simulated.
32 devices in a mesh: gx: 2 (over core), gy: 4 (over y, x), gz: 4 (over z).
Axes of the slice: x: 2, y: 2, z: 4, core: 2. Of those that a mesh axis runs over, the one named last changes fastest.
Arguments:
- flexibility: bfloat16 [4, 4, 4, 1536, 1536], P('gx', 'gy', 'gz'), may hold values from -3 to 3, as said below
- dual_load: float32 [4, 4, 4, 3, 256, 128], P('gx', 'gy', 'gz'), may hold values from -20 to 20
- coarse_load: float32 [4, 4, 4, 128], replicated, may hold values from -384 to 384
- glue: int32 [4, 4, 4, 3], replicated, may hold values 0 or 1
- floating_flag: int32 [4, 4, 4], replicated, may hold values 0 or 1
Outputs:
- multipliers: float32 [4, 4, 4, 3, 256, 128], P('gx', 'gy', 'gz')
- residual: float32 [4, 4, 4, 3, 256, 128], P('gx', 'gy', 'gz')
Inputs may be any that keep to these rules, and one draw needn't show every extreme that they name: `flexibility`: for every subdomain the [1536, 1536] matrix is symmetric and positive definite.
All inputs are finite; a program needn't handle non-finite values.
Results may differ from a plain program's by a relative error of at most 0.015.
Values sent between devices are 32-bit elements; how exact they have to be, the bound alone decides.
A program may use at most 128 MiB of HBM per device.

v0:
```python
import math
import jax
import jax.numpy as jnp
from jax import lax
from jax.sharding import PartitionSpec as P

ITERS = 4


def padded_2(cells, sides, width):
    for axis, dim in sides:
        count = lax.axis_size(axis)
        ends = count - 1
        head = lax.slice_in_dim(cells, 0, width, axis=dim)
        tail = lax.slice_in_dim(cells, cells.shape[dim] - width, cells.shape[dim], axis=dim)
        cells = jnp.concatenate(
            [
                lax.ppermute(tail, axis, [(i, (i + 1) % count) for i in range(ends)]),
                cells,
                lax.ppermute(head, axis, [((i + 1) % count, i) for i in range(ends)]),
            ],
            axis=dim,
        )
    return cells


def shifted(values, dimension, toward):
    length = values.shape[dimension]
    widths = [(0, 0)] * values.ndim
    if toward > 0:
        widths[dimension] = (0, 1)
        return lax.slice_in_dim(jnp.pad(values, widths), 1, length + 1, axis=dimension)
    widths[dimension] = (1, 0)
    return lax.slice_in_dim(jnp.pad(values, widths), 0, length, axis=dimension)


def coupling(glue, floating_flag):
    grid_shape = floating_flag.shape
    active = []
    for dimension in range(3):
        coordinate = lax.broadcasted_iota(jnp.int32, grid_shape, dimension)
        inside = (coordinate < grid_shape[dimension] - 1).astype(jnp.int32)
        active.append(inside * glue[..., dimension])
    return (jnp.stack(active, axis=-1), floating_flag)


def coarse_matrix(active, floating):
    grid_shape = floating.shape
    total_count = grid_shape[0] * grid_shape[1] * grid_shape[2]
    strides = (grid_shape[1] * grid_shape[2], grid_shape[2], 1)
    support = 2.0 / float(grid_shape[0] * grid_shape[0])
    degree = jnp.zeros(grid_shape, jnp.int32)
    for dimension in range(3):
        degree = degree + active[..., dimension] + shifted(active[..., dimension], dimension, -1)
    flat_float = floating.reshape(total_count).astype(jnp.float32)
    diagonal = jnp.where(
        flat_float > 0, degree.reshape(total_count).astype(jnp.float32) + support, 1.0
    )
    row_index = lax.broadcasted_iota(jnp.int32, (total_count, total_count), 0)
    col_index = lax.broadcasted_iota(jnp.int32, (total_count, total_count), 1)
    matrix = jnp.where(row_index == col_index, diagonal[:, None], 0.0)
    for dimension in range(3):
        link_weight = (
            (active[..., dimension] * floating * shifted(floating, dimension, 1))
            .reshape(total_count)
            .astype(jnp.float32)
        )
        upper_band = jnp.where(
            col_index == row_index + strides[dimension], link_weight[:, None], 0.0
        )
        matrix = matrix - upper_band - upper_band.T
    return matrix


def alternate(low_part, high_part, dimension):
    joined = jnp.stack([low_part, high_part], axis=dimension + 1)
    new_shape = (
        low_part.shape[:dimension]
        + (2 * low_part.shape[dimension],)
        + low_part.shape[dimension + 1 :]
    )
    return joined.reshape(new_shape)


def separate(padded, dimension, layers):
    from_above = lax.slice_in_dim(padded, 3, 2 * layers + 2, stride=2, axis=dimension)
    from_below = lax.slice_in_dim(padded, 0, 2 * layers, stride=2, axis=dimension)
    return (from_above, from_below)


def per_device(flexibility, dual_load, coarse_load, glue, floating_flag):
    block_x, block_y, block_z = (dual_load.shape[0], dual_load.shape[1], dual_load.shape[2])
    face_dofs, cases = (dual_load.shape[4], dual_load.shape[5])
    grid_x, grid_y, grid_z = floating_flag.shape
    subdomains = grid_x * grid_y * grid_z
    local_count = block_x * block_y * block_z
    start_x = lax.axis_index("gx") * block_x
    start_y = lax.axis_index("gy") * block_y
    start_z = lax.axis_index("gz") * block_z
    active_int, floating_int = coupling(glue, floating_flag)
    factor = jnp.linalg.cholesky(coarse_matrix(active_int, floating_int))
    mode_value = 1.0 / math.sqrt(face_dofs)
    support_value = 2.0 / float(grid_x * grid_x)
    active_global = active_int.astype(jnp.float32)
    below_global = jnp.stack(
        [shifted(active_global[..., dimension], dimension, -1) for dimension in range(3)], axis=-1
    )
    floating_global = floating_int.astype(jnp.float32)
    full_shape = (block_x, block_y, block_z, 3, face_dofs, cases)

    def own_block(values):
        return lax.dynamic_slice(
            values,
            (start_x, start_y, start_z) + (0,) * (values.ndim - 3),
            (block_x, block_y, block_z) + values.shape[3:],
        )

    upper_active = own_block(active_global)
    lower_active = own_block(below_global)
    upper_mask = upper_active[..., None, None]
    lower_mask = lower_active[..., None, None]
    floating_block = own_block(floating_global)
    matrices = flexibility.reshape(local_count, 6 * face_dofs, 6 * face_dofs)

    def operate(upper_part, lower_part, offset):
        face_list = []
        for dimension in range(3):
            face_list.append(-lower_part[:, :, :, dimension])
            face_list.append(upper_part[:, :, :, dimension])
        face_loads = (
            jnp.stack(face_list, axis=3)
            .astype(jnp.bfloat16)
            .reshape(local_count, 6 * face_dofs, cases)
        )
        traces = jnp.einsum(
            "sij,sjr->sir", matrices, face_loads, preferred_element_type=jnp.float32
        )
        traces = traces.reshape(block_x, block_y, block_z, 6, face_dofs, cases)
        low_face = traces[:, :, :, 0::2]
        high_face = traces[:, :, :, 1::2] - offset
        padded_x = padded_2(
            alternate(low_face[:, :, :, 0], high_face[:, :, :, 0], 0), (("gx", 0),), 1
        )
        above_x, below_x = separate(padded_x, 0, block_x)
        padded_y = padded_2(
            alternate(low_face[:, :, :, 1], high_face[:, :, :, 1], 1), (("gy", 1),), 1
        )
        above_y, below_y = separate(padded_y, 1, block_y)
        padded_z = padded_2(
            alternate(low_face[:, :, :, 2], high_face[:, :, :, 2], 2), (("gz", 2),), 1
        )
        above_z, below_z = separate(padded_z, 2, block_z)
        upper_jump = upper_mask * (high_face - jnp.stack([above_x, above_y, above_z], axis=3))
        lower_jump = lower_mask * (jnp.stack([below_x, below_y, below_z], axis=3) - low_face)
        return (upper_jump, lower_jump)

    def coarse_solve(source):
        return jax.scipy.linalg.cho_solve(
            (factor, True), source.reshape(subdomains, cases)
        ).reshape(grid_x, grid_y, grid_z, cases)

    def correction(amplitude):
        padded = jnp.pad(amplitude, ((1, 1), (1, 1), (1, 1), (0, 0)))
        window = lax.dynamic_slice(
            padded, (start_x, start_y, start_z, 0), (block_x + 2, block_y + 2, block_z + 2, cases)
        )
        centre = window[1:-1, 1:-1, 1:-1]
        upward = [window[2:, 1:-1, 1:-1], window[1:-1, 2:, 1:-1], window[1:-1, 1:-1, 2:]]
        downward = [window[:-2, 1:-1, 1:-1], window[1:-1, :-2, 1:-1], window[1:-1, 1:-1, :-2]]
        upper_part = jnp.stack(
            [
                upper_active[..., dimension, None] * mode_value * (centre - upward[dimension])
                for dimension in range(3)
            ],
            axis=3,
        )
        lower_part = jnp.stack(
            [
                lower_active[..., dimension, None] * mode_value * (downward[dimension] - centre)
                for dimension in range(3)
            ],
            axis=3,
        )
        return (upper_part[:, :, :, :, None, :], lower_part[:, :, :, :, None, :])

    def assemble(block):
        canvas = jnp.zeros((grid_x, grid_y, grid_z, cases), jnp.float32)
        canvas = lax.dynamic_update_slice(canvas, block, (start_x, start_y, start_z, 0))
        arranged = lax.psum(canvas, ("gx", "gy", "gz"))
        return arranged

    def coarse_source(upper_part, lower_part):
        return (
            mode_value * floating_block[..., None] * jnp.sum(upper_part - lower_part, axis=(3, 4))
        )

    def inner_sums(left, right):
        return jnp.sum(left * right, axis=(0, 1, 2, 3, 4))

    def projected_norm(squared_value, source_value, amplitude_value):
        removed = jnp.sum(source_value * amplitude_value, axis=(0, 1, 2))
        removed = removed + support_value * jnp.sum(
            amplitude_value * amplitude_value, axis=(0, 1, 2)
        )
        return squared_value - removed

    def totals(stacked):
        return lax.psum(stacked, ("gx", "gy", "gz"))

    start_amplitude = coarse_solve(floating_global[..., None] * coarse_load)
    spread_upper, spread_lower = correction(start_amplitude)
    multiplier_upper = jnp.broadcast_to(spread_upper, full_shape)
    multiplier_lower = jnp.broadcast_to(spread_lower, full_shape)
    jump_upper, jump_lower = operate(multiplier_upper, multiplier_lower, dual_load)
    residual_upper = -jump_upper
    residual_lower = -jump_lower
    source = assemble(coarse_source(residual_upper, residual_lower))
    squared = totals(inner_sums(residual_upper, residual_upper)[None])[0]
    amplitude = coarse_solve(source)
    spread_upper, spread_lower = correction(amplitude)
    projected_upper = residual_upper - spread_upper
    projected_lower = residual_lower - spread_lower
    current = projected_norm(squared, source, amplitude)
    search_upper, search_lower = (projected_upper, projected_lower)
    for iteration in range(ITERS):
        applied_upper, applied_lower = operate(search_upper, search_lower, 0.0)
        partial_sums = totals(
            jnp.stack(
                [
                    inner_sums(search_upper, applied_upper),
                    inner_sums(residual_upper, applied_upper),
                    inner_sums(applied_upper, applied_upper),
                ]
            )
        )
        curvature = partial_sums[0]
        step_size = current / curvature
        multiplier_upper = multiplier_upper + step_size * search_upper
        multiplier_lower = multiplier_lower + step_size * search_lower
        residual_upper = residual_upper - step_size * applied_upper
        residual_lower = residual_lower - step_size * applied_lower
        source = assemble(coarse_source(residual_upper, residual_lower))
        amplitude = coarse_solve(source)
        spread_upper, spread_lower = correction(amplitude)
        projected_upper = residual_upper - spread_upper
        projected_lower = residual_lower - spread_lower
        squared = (
            squared - 2.0 * step_size * partial_sums[1] + step_size * step_size * partial_sums[2]
        )
        renewed = projected_norm(squared, source, amplitude)
        if iteration + 1 < ITERS:
            ratio = renewed / current
            search_upper = projected_upper + ratio * search_upper
            search_lower = projected_lower + ratio * search_lower
            current = renewed
    return (multiplier_upper, projected_upper)


def solution(mesh):
    return jax.shard_map(
        per_device,
        mesh=mesh,
        in_specs=(
            P("gx", "gy", "gz", None, None),
            P("gx", "gy", "gz", None, None, None),
            P(),
            P(),
            P(),
        ),
        out_specs=(P("gx", "gy", "gz", None, None, None), P("gx", "gy", "gz", None, None, None)),
        check_vma=False,
    )
```

profile of v0, /device:TPU:0, one launch (start us, length us, event | category | flops | bytes accessed | tf_op | source)
XLA Modules:
  0.0 567.9 jit_solution(11340886455706647938)
XLA Ops:
  3.8 5.8 %cholesky.19 = f32[64,64]{1,0:T(8,128)S(1)} custom-call(f32[64,64]{1,0:T(8,128)S(1)} %fusion.69), custom_call_target="Cholesky" | custom-call | tf_op jit(solution)/shard_map/jit(cholesky)/cholesky | solution.py:101
  10.9 4.9 custom-call.13
  18.1 6.9 %fusion.10 = f32[2,1536,128]{1,2,0:T(8,128)S(1)} fusion(bf16[2,1536,128]{2,1,0:T(8,128)(2,1)S(1)} %bitcast.457, bf16[2,1,1,1536,1536]{4,3,2,1,0:T(8,128)(2,1)} %param.7), kind=kOutput, calls=%fused_computation.10 | convolution fusion | flops 1207959552 | bytes 11796480 | tf_op jit(solution)/shard_map/sij,sjr->sir/dot_general | solution.py:135
  28.4 3.0 collective-permute-start
  34.9 5.5 collective-permute-start.4
  43.0 4.6 collective-permute-start.5
  48.7 3.4 collective-permute-done.3
  52.1 2.2 collective-permute-done.5
  54.3 1.6 subtract_reduce_fusion.3
  56.1 41.0 %psum.71 = f32[4,4,4,128]{3,2,1,0:T(4,128)S(1)} all-reduce(f32[4,4,4,128]{3,2,1,0:T(4,128)S(1)} %dynamic_update_slice.15), channel_id=1, replica_groups=mesh['gx'=2,'gy'=4,'gz'=4] {'gx','gy','gz'}, use_global_device_ids=true, to_apply=%region_5.7 | all-reduce | flops 8192 | bytes 65536 | tf_op jit(solution)/shard_map/psum | solution.py:189
  98.6 6.9 %fusion.13 = f32[2,1536,128]{1,2,0:T(8,128)S(1)} fusion(bf16[2,1536,128]{2,1,0:T(8,128)(2,1)S(1)} %bitcast.458, bf16[2,1,1,1536,1536]{4,3,2,1,0:T(8,128)(2,1)} %param.7), kind=kOutput, calls=%fused_computation.11 | convolution fusion | flops 1207959552 | bytes 11796480 | tf_op jit(solution)/shard_map/sij,sjr->sir/dot_general | solution.py:135
  105.5 1.6 copy.84
  107.2 1.5 fusion.150
  115.6 5.5 collective-permute-start.10
  121.7 5.3 collective-permute-start.11
  127.5 40.5 %all-reduce.15 = (f32[3,128]{1,0:T(4,128)S(1)}, f32[128]{0:T(128)S(1)}) all-reduce(f32[3,128]{1,0:T(4,128)S(1)} %pad_maximum_fusion.14, f32[128]{0:T(128)S(1)} %get-tuple-element.19), channel_id=1, replica_groups=mesh['gx'=2,'gy'=4,'gz'=4] {'gx','gy','gz'}, use_global_device_ids=true, to_apply=%region_11.13 | all-reduce | flops 512 | bytes 4096 | tf_op jit(solution)/shard_map/psum | solution.py:208
  168.0 2.8 subtract_reduce_fusion.2
  170.9 39.8 %psum.73 = f32[4,4,4,128]{3,2,1,0:T(4,128)S(1)} all-reduce(f32[4,4,4,128]{3,2,1,0:T(4,128)S(1)} %dynamic_update_slice.16), channel_id=1, replica_groups=mesh['gx'=2,'gy'=4,'gz'=4] {'gx','gy','gz'}, use_global_device_ids=true, to_apply=%region_13.15 | all-reduce | flops 8192 | bytes 65536 | tf_op jit(solution)/shard_map/psum | solution.py:189
  211.4 1.7 fusion.142
  214.0 8.1 %fusion.16 = f32[2,1536,128]{1,2,0:T(8,128)} fusion(bf16[2,1536,128]{2,1,0:T(8,128)(2,1)S(1)} %bitcast.460, bf16[2,1,1,1536,1536]{4,3,2,1,0:T(8,128)(2,1)} %param.7), kind=kOutput, calls=%fused_computation.12 | convolution fusion | flops 1207959552 | bytes 11796480 | tf_op jit(solution)/shard_map/sij,sjr->sir/dot_general | solution.py:135
  222.1 1.9 copy.97
  226.1 1.3 collective-permute-start.12
  230.9 1.4 collective-permute-start.15
  232.3 5.5 collective-permute-start.16
  237.8 5.3 collective-permute-start.17
  244.4 41.1 %psum.74 = f32[3,128]{1,0:T(4,128)S(1)} all-reduce(f32[3,128]{1,0:T(4,128)S(1)} %pad_maximum_fusion.15), channel_id=1, replica_groups=mesh['gx'=2,'gy'=4,'gz'=4] {'gx','gy','gz'}, use_global_device_ids=true, to_apply=%region_19.21 | all-reduce | flops 384 | bytes 3072 | tf_op jit(solution)/shard_map/psum | solution.py:208
  285.5 2.9 subtract_reduce_fusion.1
  288.5 40.0 %psum.75 = f32[4,4,4,128]{3,2,1,0:T(4,128)S(1)} all-reduce(f32[4,4,4,128]{3,2,1,0:T(4,128)S(1)} %dynamic_update_slice.17), channel_id=1, replica_groups=mesh['gx'=2,'gy'=4,'gz'=4] {'gx','gy','gz'}, use_global_device_ids=true, to_apply=%region_21.23 | all-reduce | flops 8192 | bytes 65536 | tf_op jit(solution)/shard_map/psum | solution.py:189
  329.3 1.6 fusion.137
  331.8 8.0 %fusion.19 = f32[2,1536,128]{1,2,0:T(8,128)} fusion(bf16[2,1536,128]{2,1,0:T(8,128)(2,1)S(1)} %bitcast.461, bf16[2,1,1,1536,1536]{4,3,2,1,0:T(8,128)(2,1)} %param.7), kind=kOutput, calls=%fused_computation.13 | convolution fusion | flops 1207959552 | bytes 11796480 | tf_op jit(solution)/shard_map/sij,sjr->sir/dot_general | solution.py:135
  339.8 3.0 copy.109
  342.9 1.5 fusion.148
  344.6 1.3 collective-permute-start.18
  351.4 5.5 collective-permute-start.22
  356.9 5.2 collective-permute-start.23
  363.7 40.4 %psum.76 = f32[3,128]{1,0:T(4,128)S(1)} all-reduce(f32[3,128]{1,0:T(4,128)S(1)} %pad_maximum_fusion.16), channel_id=1, replica_groups=mesh['gx'=2,'gy'=4,'gz'=4] {'gx','gy','gz'}, use_global_device_ids=true, to_apply=%region_27.29 | all-reduce | flops 384 | bytes 3072 | tf_op jit(solution)/shard_map/psum | solution.py:208
  404.1 3.2 subtract_reduce_fusion
  407.5 39.8 %psum.77 = f32[4,4,4,128]{3,2,1,0:T(4,128)S(1)} all-reduce(f32[4,4,4,128]{3,2,1,0:T(4,128)S(1)} %dynamic_update_slice.18), channel_id=1, replica_groups=mesh['gx'=2,'gy'=4,'gz'=4] {'gx','gy','gz'}, use_global_device_ids=true, to_apply=%region_29.31 | all-reduce | flops 8192 | bytes 65536 | tf_op jit(solution)/shard_map/psum | solution.py:189
  448.0 1.6 fusion.66
  449.8 8.1 %fusion.22 = f32[2,1536,128]{1,2,0:T(8,128)} fusion(bf16[2,1536,128]{2,1,0:T(8,128)(2,1)S(1)} %bitcast.459, bf16[2,1,1,1536,1536]{4,3,2,1,0:T(8,128)(2,1)} %param.7), kind=kOutput, calls=%fused_computation.14 | convolution fusion | flops 1207959552 | bytes 11796480 | tf_op jit(solution)/shard_map/sij,sjr->sir/dot_general | solution.py:135
  457.8 3.0 copy.122
  460.9 1.5 fusion.147
  469.3 5.5 collective-permute-start.28
  474.8 5.2 collective-permute-start.29
  481.7 40.6 %psum.78 = f32[3,128]{1,0:T(4,128)S(1)} all-reduce(f32[3,128]{1,0:T(4,128)S(1)} %pad_maximum_fusion.17), channel_id=1, replica_groups=mesh['gx'=2,'gy'=4,'gz'=4] {'gx','gy','gz'}, use_global_device_ids=true, to_apply=%region_35.37 | all-reduce | flops 384 | bytes 3072 | tf_op jit(solution)/shard_map/psum | solution.py:208
  522.4 2.1 fusion.31
  524.6 39.8 %psum.79 = f32[64,128]{1,0:T(8,128)S(1)} all-reduce(f32[64,128]{1,0:T(8,128)S(1)} %bitcast.490), channel_id=1, replica_groups=mesh['gx'=2,'gy'=4,'gz'=4] {'gx','gy','gz'}, use_global_device_ids=true, to_apply=%region_37.39 | all-reduce | flops 8192 | bytes 65536 | tf_op jit(solution)/shard_map/psum | solution.py:189
  565.0 3.0 subtract_bitcast_fusion
  (294 shorter events, 53.9 us)
Async XLA Ops:
  25.4 1.1 copy-start.13
  26.7 0.9 copy-start.5
  28.4 14.6 %collective-permute-start = (f32[1,1,1,256,128]{4,3,0,2,1:T(8,128)}, f32[1,1,1,256,128]{4,3,0,2,1:T(8,128)}, u32[]{:S(2)}, u32[]{:S(2)}) collective-permute-start(f32[1,1,1,256,128]{4,3,0,2,1:T(8,128)} %get-tuple-element.151), channel_id=1, source_target_pairs={{0,16},{1,17},{2,18},{3,19},{4,20},{5,21},{6,22},{7,23},{8,24},{9,... | collective-permute-start | bytes 393224 | tf_op jit(solution)/shard_map/ppermute | solution.py:18
  31.4 16.2 %collective-permute-start.1 = (f32[1,1,1,256,128]{4,3,0,2,1:T(8,128)}, f32[1,1,1,256,128]{4,3,0,2,1:T(8,128)}, u32[]{:S(2)}, u32[]{:S(2)}) collective-permute-start(f32[1,1,1,256,128]{4,3,0,2,1:T(8,128)} %get-tuple-element.152), channel_id=1, source_target_pairs={{16,0},{17,1},{18,2},{19,3},{20,4},{21,5},{22,6},{23,7},{24,8},{25... | collective-permute-start | bytes 393224 | tf_op jit(solution)/shard_map/ppermute | solution.py:20
  33.6 15.1 %collective-permute-start.2 = (f32[2,1,1,256,128]{4,3,0,2,1:T(8,128)}, f32[2,1,1,256,128]{4,3,0,2,1:T(8,128)S(1)}, u32[]{:S(2)}, u32[]{:S(2)}) collective-permute-start(f32[2,1,1,256,128]{4,3,0,2,1:T(8,128)} %get-tuple-element.148), channel_id=1, source_target_pairs={{4,0},{8,4},{12,8},{5,1},{9,5},{13,9},{6,2},{10,6},{14,10},{7,3},{... | collective-permute-start | bytes 786440 | tf_op jit(solution)/shard_map/ppermute | solution.py:20
  34.9 13.8 %collective-permute-start.4 = (f32[2,1,1,256,128]{4,3,0,2,1:T(8,128)}, f32[2,1,1,256,128]{4,3,0,2,1:T(8,128)}, u32[]{:S(2)}, u32[]{:S(2)}) collective-permute-start(f32[2,1,1,256,128]{4,3,0,2,1:T(8,128)} %get-tuple-element.147), channel_id=1, source_target_pairs={{0,4},{4,8},{8,12},{1,5},{5,9},{9,13},{2,6},{6,10},{10,14},{3,7},{... | collective-permute-start | bytes 786440 | tf_op jit(solution)/shard_map/ppermute | solution.py:18
  41.3 10.8 %collective-permute-start.3 = (f32[2,1,1,256,128]{4,3,0,2,1:T(8,128)}, f32[2,1,1,256,128]{4,3,0,2,1:T(8,128)S(1)}, u32[]{:S(2)}, u32[]{:S(2)}) collective-permute-start(f32[2,1,1,256,128]{4,3,0,2,1:T(8,128)} %get-tuple-element.150), channel_id=1, source_target_pairs={{1,0},{2,1},{3,2},{5,4},{6,5},{7,6},{9,8},{10,9},{11,10},{13,12},{... | collective-permute-start | bytes 786440 | tf_op jit(solution)/shard_map/ppermute | solution.py:20
  43.0 11.4 %collective-permute-start.5 = (f32[2,1,1,256,128]{4,3,0,2,1:T(8,128)}, f32[2,1,1,256,128]{4,3,0,2,1:T(8,128)S(1)}, u32[]{:S(2)}, u32[]{:S(2)}) collective-permute-start(f32[2,1,1,256,128]{4,3,0,2,1:T(8,128)} %get-tuple-element.149), channel_id=1, source_target_pairs={{0,1},{1,2},{2,3},{4,5},{5,6},{6,7},{8,9},{9,10},{10,11},{12,13},{... | collective-permute-start | bytes 786440 | tf_op jit(solution)/shard_map/ppermute | solution.py:18
  52.1 2.2 copy-start.14
  108.9 12.8 %collective-permute-start.6 = (f32[1,1,1,256,128]{4,3,0,2,1:T(8,128)S(1)}, f32[1,1,1,256,128]{4,3,0,2,1:T(8,128)S(1)}, u32[]{:S(2)}, u32[]{:S(2)}) collective-permute-start(f32[1,1,1,256,128]{4,3,0,2,1:T(8,128)S(1)} %get-tuple-element.145), channel_id=1, source_target_pairs={{0,16},{1,17},{2,18},{3,19},{4,20},{5,21},{6,22},{7,23},{8,24},{9,... | collective-permute-start | bytes 393224 | tf_op jit(solution)/shard_map/ppermute | solution.py:18
  110.2 16.8 %collective-permute-start.7 = (f32[1,1,1,256,128]{4,3,0,2,1:T(8,128)S(1)}, f32[1,1,1,256,128]{4,3,0,2,1:T(8,128)S(1)}, u32[]{:S(2)}, u32[]{:S(2)}) collective-permute-start(f32[1,1,1,256,128]{4,3,0,2,1:T(8,128)S(1)} %get-tuple-element.146), channel_id=1, source_target_pairs={{16,0},{17,1},{18,2},{19,3},{20,4},{21,5},{22,6},{23,7},{24,8},{25... | collective-permute-start | bytes 393224 | tf_op jit(solution)/shard_map/ppermute | solution.py:20
  112.3 14.8 %collective-permute-start.8 = (f32[2,1,1,256,128]{4,3,0,2,1:T(8,128)S(1)}, f32[2,1,1,256,128]{4,3,0,2,1:T(8,128)S(1)}, u32[]{:S(2)}, u32[]{:S(2)}) collective-permute-start(f32[2,1,1,256,128]{4,3,0,2,1:T(8,128)S(1)} %get-tuple-element.142), channel_id=1, source_target_pairs={{4,0},{8,4},{12,8},{5,1},{9,5},{13,9},{6,2},{10,6},{14,10},{7,3},{... | collective-permute-start | bytes 786440 | tf_op jit(solution)/shard_map/ppermute | solution.py:20
  114.3 12.8 %collective-permute-start.9 = (f32[2,1,1,256,128]{4,3,0,2,1:T(8,128)S(1)}, f32[2,1,1,256,128]{4,3,0,2,1:T(8,128)S(1)}, u32[]{:S(2)}, u32[]{:S(2)}) collective-permute-start(f32[2,1,1,256,128]{4,3,0,2,1:T(8,128)S(1)} %get-tuple-element.144), channel_id=1, source_target_pairs={{1,0},{2,1},{3,2},{5,4},{6,5},{7,6},{9,8},{10,9},{11,10},{13,12},{... | collective-permute-start | bytes 786440 | tf_op jit(solution)/shard_map/ppermute | solution.py:20
  115.6 52.4 %collective-permute-start.10 = (f32[2,1,1,256,128]{4,3,0,2,1:T(8,128)}, f32[2,1,1,256,128]{4,3,0,2,1:T(8,128)}, u32[]{:S(2)}, u32[]{:S(2)}) collective-permute-start(f32[2,1,1,256,128]{4,3,0,2,1:T(8,128)} %get-tuple-element.141), channel_id=1, source_target_pairs={{0,4},{4,8},{8,12},{1,5},{5,9},{9,13},{2,6},{6,10},{10,14},{3,7},{... | collective-permute-start | bytes 786440 | tf_op jit(solution)/shard_map/ppermute | solution.py:18
  121.7 46.3 %collective-permute-start.11 = (f32[2,1,1,256,128]{4,3,2,0,1:T(8,128)}, f32[2,1,1,256,128]{4,3,2,0,1:T(8,128)}, u32[]{:S(2)}, u32[]{:S(2)}) collective-permute-start(f32[2,1,1,256,128]{4,3,2,0,1:T(8,128)} %get-tuple-element.143), channel_id=1, source_target_pairs={{0,1},{1,2},{2,3},{4,5},{5,6},{6,7},{8,9},{9,10},{10,11},{12,13},{... | collective-permute-start | bytes 786440 | tf_op jit(solution)/shard_map/ppermute | solution.py:18
  127.0 41.0 %copy-start.19 = (f32[128]{0:T(128)S(1)}, f32[128]{0:T(128)}, u32[]{:S(2)}) copy-start(f32[128]{0:T(128)} %get-tuple-element.208) | copy-start | bytes 1540
  127.0 41.0 %copy-start.20 = (f32[128]{0:T(128)S(1)}, f32[128]{0:T(128)}, u32[]{:S(2)}) copy-start(f32[128]{0:T(128)} %multiply_reduce_fusion.20) | copy-start | bytes 1540
  168.0 43.4 %copy-start.15 = (f32[128]{0:T(128)}, f32[128]{0:T(128)S(1)}, u32[]{:S(2)}) copy-start(f32[128]{0:T(128)S(1)} %bitcast_divide_fusion.3) | copy-start | bytes 1540
  213.1 0.9 copy-start.8
  213.1 116.1 %copy-start.1 = (f32[2,1,1,3,256,128]{5,4,3,0,2,1:T(8,128)}, f32[2,1,1,3,256,128]{5,4,3,0,2,1:T(8,128)S(1)}, u32[]{:S(2)}) copy-start(f32[2,1,1,3,256,128]{5,4,3,0,2,1:T(8,128)S(1)} %get-tuple-element.49) | copy-start | bytes 2359300
  223.9 1.2 copy-start.3
  225.1 0.9 copy-start.7
  226.1 11.7 %collective-permute-start.12 = (f32[1,1,1,256,128]{4,3,0,2,1:T(8,128)S(1)}, f32[1,1,1,256,128]{4,3,0,2,1:T(8,128)S(1)}, u32[]{:S(2)}, u32[]{:S(2)}) collective-permute-start(f32[1,1,1,256,128]{4,3,0,2,1:T(8,128)S(1)} %get-tuple-element.139), channel_id=1, source_target_pairs={{0,16},{1,17},{2,18},{3,19},{4,20},{5,21},{6,22},{7,23},{8,24},{9,... | collective-permute-start | bytes 393224 | tf_op jit(solution)/shard_map/ppermute | solution.py:18
  227.4 15.7 %collective-permute-start.13 = (f32[1,1,1,256,128]{4,3,0,2,1:T(8,128)S(1)}, f32[1,1,1,256,128]{4,3,0,2,1:T(8,128)S(1)}, u32[]{:S(2)}, u32[]{:S(2)}) collective-permute-start(f32[1,1,1,256,128]{4,3,0,2,1:T(8,128)S(1)} %get-tuple-element.140), channel_id=1, source_target_pairs={{16,0},{17,1},{18,2},{19,3},{20,4},{21,5},{22,6},{23,7},{24,8},{25... | collective-permute-start | bytes 393224 | tf_op jit(solution)/shard_map/ppermute | solution.py:20
  229.5 13.7 %collective-permute-start.14 = (f32[2,1,1,256,128]{4,3,0,1,2:T(8,128)S(1)}, f32[2,1,1,256,128]{4,3,0,1,2:T(8,128)S(1)}, u32[]{:S(2)}, u32[]{:S(2)}) collective-permute-start(f32[2,1,1,256,128]{4,3,0,1,2:T(8,128)S(1)} %get-tuple-element.135), channel_id=1, source_target_pairs={{4,0},{8,4},{12,8},{5,1},{9,5},{13,9},{6,2},{10,6},{14,10},{7,3},{... | collective-permute-start | bytes 786440 | tf_op jit(solution)/shard_map/ppermute | solution.py:20
  230.9 12.3 %copy-start.2 = (f32[2,1,1,3,256,128]{5,4,3,0,2,1:T(8,128)S(1)}, f32[2,1,1,3,256,128]{5,4,3,0,2,1:T(8,128)}, u32[]{:S(2)}) copy-start(f32[2,1,1,3,256,128]{5,4,3,0,2,1:T(8,128)} %get-tuple-element.57) | copy-start | bytes 2359300
  230.9 12.3 %copy-start.4 = (f32[2,1536,128]{2,1,0:T(8,128)S(1)}, f32[2,1536,128]{2,1,0:T(8,128)}, u32[]{:S(2)}) copy-start(f32[2,1536,128]{2,1,0:T(8,128)} %copy-done.3) | copy-start | bytes 4718596
  230.9 12.3 %collective-permute-start.15 = (f32[2,1,1,256,128]{4,3,0,2,1:T(8,128)S(1)}, f32[2,1,1,256,128]{4,3,0,2,1:T(8,128)S(1)}, u32[]{:S(2)}, u32[]{:S(2)}) collective-permute-start(f32[2,1,1,256,128]{4,3,0,2,1:T(8,128)S(1)} %get-tuple-element.137), channel_id=1, source_target_pairs={{1,0},{2,1},{3,2},{5,4},{6,5},{7,6},{9,8},{10,9},{11,10},{13,12},{... | collective-permute-start | bytes 786440 | tf_op jit(solution)/shard_map/ppermute | solution.py:20
  232.3 53.2 %collective-permute-start.16 = (f32[2,1,1,256,128]{4,3,0,1,2:T(8,128)}, f32[2,1,1,256,128]{4,3,0,1,2:T(8,128)}, u32[]{:S(2)}, u32[]{:S(2)}) collective-permute-start(f32[2,1,1,256,128]{4,3,0,1,2:T(8,128)} %get-tuple-element.136), channel_id=1, source_target_pairs={{0,4},{4,8},{8,12},{1,5},{5,9},{9,13},{2,6},{6,10},{10,14},{3,7},{... | collective-permute-start | bytes 786440 | tf_op jit(solution)/shard_map/ppermute | solution.py:18
  237.8 47.7 %collective-permute-start.17 = (f32[2,1,1,256,128]{4,3,0,2,1:T(8,128)S(1)}, f32[2,1,1,256,128]{4,3,0,2,1:T(8,128)}, u32[]{:S(2)}, u32[]{:S(2)}) collective-permute-start(f32[2,1,1,256,128]{4,3,0,2,1:T(8,128)S(1)} %get-tuple-element.138), channel_id=1, source_target_pairs={{0,1},{1,2},{2,3},{4,5},{5,6},{6,7},{8,9},{9,10},{10,11},{12,13},{... | collective-permute-start | bytes 786440 | tf_op jit(solution)/shard_map/ppermute | solution.py:18
  285.5 43.7 %copy-start.21 = (f32[128]{0:T(128)}, f32[128]{0:T(128)S(1)}, u32[]{:S(2)}) copy-start(f32[128]{0:T(128)S(1)} %bitcast_divide_fusion.2) | copy-start | bytes 1540
  288.4 74.5 %copy-start = (f32[2,1,1,3,256,128]{5,4,3,0,2,1:T(8,128)}, f32[2,1,1,3,256,128]{5,4,3,0,2,1:T(8,128)S(1)}, u32[]{:S(2)}) copy-start(f32[2,1,1,3,256,128]{5,4,3,0,2,1:T(8,128)S(1)} %get-tuple-element.46) | copy-start | bytes 2359300
  344.6 12.3 %collective-permute-start.18 = (f32[1,1,1,256,128]{4,3,0,2,1:T(8,128)S(1)}, f32[1,1,1,256,128]{4,3,0,2,1:T(8,128)S(1)}, u32[]{:S(2)}, u32[]{:S(2)}) collective-permute-start(f32[1,1,1,256,128]{4,3,0,2,1:T(8,128)S(1)} %get-tuple-element.133), channel_id=1, source_target_pairs={{0,16},{1,17},{2,18},{3,19},{4,20},{5,21},{6,22},{7,23},{8,24},{9,... | collective-permute-start | bytes 393224 | tf_op jit(solution)/shard_map/ppermute | solution.py:18
  345.9 16.2 %collective-permute-start.19 = (f32[1,1,1,256,128]{4,3,0,2,1:T(8,128)S(1)}, f32[1,1,1,256,128]{4,3,0,2,1:T(8,128)S(1)}, u32[]{:S(2)}, u32[]{:S(2)}) collective-permute-start(f32[1,1,1,256,128]{4,3,0,2,1:T(8,128)S(1)} %get-tuple-element.134), channel_id=1, source_target_pairs={{16,0},{17,1},{18,2},{19,3},{20,4},{21,5},{22,6},{23,7},{24,8},{25... | collective-permute-start | bytes 393224 | tf_op jit(solution)/shard_map/ppermute | solution.py:20
  348.0 14.9 %collective-permute-start.20 = (f32[2,1,1,256,128]{4,3,0,2,1:T(8,128)S(1)}, f32[2,1,1,256,128]{4,3,0,2,1:T(8,128)S(1)}, u32[]{:S(2)}, u32[]{:S(2)}) collective-permute-start(f32[2,1,1,256,128]{4,3,0,2,1:T(8,128)S(1)} %get-tuple-element.129), channel_id=1, source_target_pairs={{4,0},{8,4},{12,8},{5,1},{9,5},{13,9},{6,2},{10,6},{14,10},{7,3},{... | collective-permute-start | bytes 786440 | tf_op jit(solution)/shard_map/ppermute | solution.py:20
  350.1 12.9 %collective-permute-start.21 = (f32[2,1,1,256,128]{4,3,0,2,1:T(8,128)S(1)}, f32[2,1,1,256,128]{4,3,0,2,1:T(8,128)S(1)}, u32[]{:S(2)}, u32[]{:S(2)}) collective-permute-start(f32[2,1,1,256,128]{4,3,0,2,1:T(8,128)S(1)} %get-tuple-element.131), channel_id=1, source_target_pairs={{1,0},{2,1},{3,2},{5,4},{6,5},{7,6},{9,8},{10,9},{11,10},{13,12},{... | collective-permute-start | bytes 786440 | tf_op jit(solution)/shard_map/ppermute | solution.py:20
  351.4 52.8 %collective-permute-start.22 = (f32[2,1,1,256,128]{4,3,0,2,1:T(8,128)}, f32[2,1,1,256,128]{4,3,0,2,1:T(8,128)}, u32[]{:S(2)}, u32[]{:S(2)}) collective-permute-start(f32[2,1,1,256,128]{4,3,0,2,1:T(8,128)} %get-tuple-element.130), channel_id=1, source_target_pairs={{0,4},{4,8},{8,12},{1,5},{5,9},{9,13},{2,6},{6,10},{10,14},{3,7},{... | collective-permute-start | bytes 786440 | tf_op jit(solution)/shard_map/ppermute | solution.py:18
  356.9 47.3 %collective-permute-start.23 = (f32[2,1,1,256,128]{4,3,2,0,1:T(8,128)}, f32[2,1,1,256,128]{4,3,2,0,1:T(8,128)}, u32[]{:S(2)}, u32[]{:S(2)}) collective-permute-start(f32[2,1,1,256,128]{4,3,2,0,1:T(8,128)} %get-tuple-element.132), channel_id=1, source_target_pairs={{0,1},{1,2},{2,3},{4,5},{5,6},{6,7},{8,9},{9,10},{10,11},{12,13},{... | collective-permute-start | bytes 786440 | tf_op jit(solution)/shard_map/ppermute | solution.py:18
  404.1 43.8 %copy-start.17 = (f32[128]{0:T(128)}, f32[128]{0:T(128)S(1)}, u32[]{:S(2)}) copy-start(f32[128]{0:T(128)S(1)} %bitcast_divide_fusion.1) | copy-start | bytes 1540
  462.6 12.3 %collective-permute-start.24 = (f32[1,1,1,256,128]{4,3,0,2,1:T(8,128)S(1)}, f32[1,1,1,256,128]{4,3,0,2,1:T(8,128)S(1)}, u32[]{:S(2)}, u32[]{:S(2)}) collective-permute-start(f32[1,1,1,256,128]{4,3,0,2,1:T(8,128)S(1)} %get-tuple-element.127), channel_id=1, source_target_pairs={{0,16},{1,17},{2,18},{3,19},{4,20},{5,21},{6,22},{7,23},{8,24},{9,... | collective-permute-start | bytes 393224 | tf_op jit(solution)/shard_map/ppermute | solution.py:18
  463.9 16.2 %collective-permute-start.25 = (f32[1,1,1,256,128]{4,3,0,2,1:T(8,128)S(1)}, f32[1,1,1,256,128]{4,3,0,2,1:T(8,128)S(1)}, u32[]{:S(2)}, u32[]{:S(2)}) collective-permute-start(f32[1,1,1,256,128]{4,3,0,2,1:T(8,128)S(1)} %get-tuple-element.128), channel_id=1, source_target_pairs={{16,0},{17,1},{18,2},{19,3},{20,4},{21,5},{22,6},{23,7},{24,8},{25... | collective-permute-start | bytes 393224 | tf_op jit(solution)/shard_map/ppermute | solution.py:20
  466.0 14.9 %collective-permute-start.26 = (f32[2,1,1,256,128]{4,3,0,2,1:T(8,128)S(1)}, f32[2,1,1,256,128]{4,3,0,2,1:T(8,128)S(1)}, u32[]{:S(2)}, u32[]{:S(2)}) collective-permute-start(f32[2,1,1,256,128]{4,3,0,2,1:T(8,128)S(1)} %get-tuple-element.124), channel_id=1, source_target_pairs={{4,0},{8,4},{12,8},{5,1},{9,5},{13,9},{6,2},{10,6},{14,10},{7,3},{... | collective-permute-start | bytes 786440 | tf_op jit(solution)/shard_map/ppermute | solution.py:20
  468.0 12.9 %collective-permute-start.27 = (f32[2,1,1,256,128]{4,3,0,2,1:T(8,128)S(1)}, f32[2,1,1,256,128]{4,3,0,2,1:T(8,128)S(1)}, u32[]{:S(2)}, u32[]{:S(2)}) collective-permute-start(f32[2,1,1,256,128]{4,3,0,2,1:T(8,128)S(1)} %get-tuple-element.126), channel_id=1, source_target_pairs={{1,0},{2,1},{3,2},{5,4},{6,5},{7,6},{9,8},{10,9},{11,10},{13,12},{... | collective-permute-start | bytes 786440 | tf_op jit(solution)/shard_map/ppermute | solution.py:20
  469.3 53.0 %collective-permute-start.28 = (f32[2,1,1,256,128]{4,3,0,2,1:T(8,128)}, f32[2,1,1,256,128]{4,3,0,2,1:T(8,128)}, u32[]{:S(2)}, u32[]{:S(2)}) collective-permute-start(f32[2,1,1,256,128]{4,3,0,2,1:T(8,128)} %get-tuple-element.123), channel_id=1, source_target_pairs={{0,4},{4,8},{8,12},{1,5},{5,9},{9,13},{2,6},{6,10},{10,14},{3,7},{... | collective-permute-start | bytes 786440 | tf_op jit(solution)/shard_map/ppermute | solution.py:18
  474.8 47.5 %collective-permute-start.29 = (f32[2,1,1,256,128]{4,3,2,0,1:T(8,128)}, f32[2,1,1,256,128]{4,3,2,0,1:T(8,128)}, u32[]{:S(2)}, u32[]{:S(2)}) collective-permute-start(f32[2,1,1,256,128]{4,3,2,0,1:T(8,128)} %get-tuple-element.125), channel_id=1, source_target_pairs={{0,1},{1,2},{2,3},{4,5},{5,6},{6,7},{8,9},{9,10},{10,11},{12,13},{... | collective-permute-start | bytes 786440 | tf_op jit(solution)/shard_map/ppermute | solution.py:18
  522.3 2.1 copy-start.22
  522.3 42.6 %copy-start.16 = (f32[128]{0:T(128)S(1)}, f32[128]{0:T(128)}, u32[]{:S(2)}) copy-start(f32[128]{0:T(128)} %copy-done.15) | copy-start | bytes 1540
  522.3 42.6 %copy-start.18 = (f32[128]{0:T(128)S(1)}, f32[128]{0:T(128)}, u32[]{:S(2)}) copy-start(f32[128]{0:T(128)} %copy-done.17) | copy-start | bytes 1540
  (5 other events, 3.9 us)
where the time goes:
time: 570 us; the launch traced here: 568 us
  blocking collectives  363 us (64%)
  starting transfers between devices  80.8 us (14%)
  other arithmetic  43.5 us (8%)
  matrix products  40.9 us (7%)
  local copies, waits for them, and re-layouts  32 us (6%)
  waiting for transfers between devices  5.72 us (1%)
    psum x5, blocking collectives, assemble(): arranged = lax.psum(canvas, ('gx', 'gy', 'gz'))  200 us
    psum x4, blocking collectives, totals(): return lax.psum(stacked, ('gx', 'gy', 'gz'))  163 us
    ppermute x15, starting transfers between devices, padded_2(): lax.ppermute(tail, axis, [(i, (i + 1) % count) for i in range(ends)])  61.4 us
    dot_general x5, matrix products, operate(): jnp.einsum('sij,sjr->sir', matrices, face_loads, preferred_element_type=j...  37.9 us
    ppermute x15, starting transfers between devices, padded_2(): lax.ppermute(head, axis, [((i + 1) % count, i) for i in range(ends)])  19.4 us
    reduce_sum x5, other arithmetic, coarse_source(): jnp.sum(upper_part - lower_part, axis=(3, 4))  12.7 us
  transfers between devices with their start and end apart: 30, of which 2 were waited for; matrix products, arithmetic and copies ran while one was open for 2% of the time, Pallas kernels for 0%

commit v1 on v0

--- a/solution.py
+++ b/solution.py
@@ -186,7 +186,8 @@
     def assemble(block):
         canvas = jnp.zeros((grid_x, grid_y, grid_z, cases), jnp.float32)
         canvas = lax.dynamic_update_slice(canvas, block, (start_x, start_y, start_z, 0))
-        arranged = lax.psum(canvas, ("gx", "gy", "gz"))
+        partial = lax.psum(canvas, ("gy", "gz"))
+        arranged = lax.psum(partial, "gx")
         return arranged
 
     def coarse_source(upper_part, lower_part):

time: 570 us -> 759 us (1.33)
  blocking collectives: 363 us -> 549 us
    psum x5 -> x10, blocking collectives: 200 us -> 395 us  [the longest x5 378 us: assemble(): partial = lax.psum(canvas, ('gy', 'gz'))]
    psum x4, blocking collectives: 163 us -> 154 us  [totals(): return lax.psum(stacked, ('gx', 'gy', 'gz'))]
where the time goes in v1:
time: 759 us; the launch traced here: 756 us
  blocking collectives  549 us (72%)
  starting transfers between devices  83.6 us (11%)
  other arithmetic  43.5 us (6%)
  matrix products  40.9 us (5%)
  local copies, waits for them, and re-layouts  32 us (4%)
    psum x5, blocking collectives, assemble(): partial = lax.psum(canvas, ('gy', 'gz'))  378 us
    psum x4, blocking collectives, totals(): return lax.psum(stacked, ('gx', 'gy', 'gz'))  154 us
    ppermute x15, starting transfers between devices, padded_2(): lax.ppermute(tail, axis, [(i, (i + 1) % count) for i in range(ends)])  64.2 us
    dot_general x5, matrix products, operate(): jnp.einsum('sij,sjr->sir', matrices, face_loads, preferred_element_type=j...  37.9 us
    ppermute x15, starting transfers between devices, padded_2(): lax.ppermute(head, axis, [((i + 1) % count, i) for i in range(ends)])  19.4 us
    psum x5, blocking collectives, assemble(): arranged = lax.psum(partial, 'gx')  17 us
  transfers between devices with their start and end apart: 30, of which 2 were waited for; matrix products, arithmetic and copies ran while one was open for 2% of the time, Pallas kernels for 0%

profile of v1, /device:TPU:0, one launch (start us, length us, event | category | flops | bytes accessed | tf_op | source)
XLA Modules:
  0.0 756.5 jit_solution(518189441359054895)
XLA Ops:
  3.8 5.8 cholesky.19
  10.9 4.9 custom-call.13
  18.1 6.9 fusion.10
  28.4 3.0 collective-permute-start
  34.9 5.5 collective-permute-start.4
  43.0 4.6 collective-permute-start.5
  48.7 3.4 collective-permute-done.3
  52.1 2.2 collective-permute-done.5
  54.3 1.6 subtract_reduce_fusion.3
  56.1 76.0 %psum.106 = f32[4,4,4,128]{3,2,1,0:T(4,128)S(1)} all-reduce(f32[4,4,4,128]{3,2,1,0:T(4,128)S(1)} %dynamic_update_slice.15), channel_id=1, replica_groups=mesh['gx'=2,'gy'=4,'gz'=4] {'gy','gz'}, use_global_device_ids=true, to_apply=%region_5.7 | all-reduce | flops 8192 | bytes 65536 | tf_op jit(solution)/shard_map/psum | solution.py:189
  132.0 3.4 psum.107
  137.0 6.9 fusion.13
  147.2 2.3 collective-permute-start.6
  154.9 5.3 collective-permute-start.10
  160.7 5.3 collective-permute-start.11
  166.6 39.9 %all-reduce.15 = (f32[3,128]{1,0:T(4,128)S(1)}, f32[128]{0:T(128)S(1)}) all-reduce(f32[3,128]{1,0:T(4,128)S(1)} %pad_maximum_fusion.14, f32[128]{0:T(128)S(1)} %get-tuple-element.19), channel_id=1, replica_groups=mesh['gx'=2,'gy'=4,'gz'=4] {'gx','gy','gz'}, use_global_device_ids=true, to_apply=%region_12.14 | all-reduce | flops 512 | bytes 4096 | tf_op jit(solution)/shard_map/psum | solution.py:209
  206.5 2.8 subtract_reduce_fusion.2
  209.4 75.3 %psum.109 = f32[4,4,4,128]{3,2,1,0:T(4,128)S(1)} all-reduce(f32[4,4,4,128]{3,2,1,0:T(4,128)S(1)} %dynamic_update_slice.16), channel_id=1, replica_groups=mesh['gx'=2,'gy'=4,'gz'=4] {'gy','gz'}, use_global_device_ids=true, to_apply=%region_14.16 | all-reduce | flops 8192 | bytes 65536 | tf_op jit(solution)/shard_map/psum | solution.py:189
  284.8 3.4 psum.110
  288.9 1.7 fusion.142
  291.4 8.0 %fusion.16 = f32[2,1536,128]{1,2,0:T(8,128)} fusion(bf16[2,1536,128]{2,1,0:T(8,128)(2,1)S(1)} %bitcast.460, bf16[2,1,1,1536,1536]{4,3,2,1,0:T(8,128)(2,1)} %param.7), kind=kOutput, calls=%fused_computation.12 | convolution fusion | flops 1207959552 | bytes 11796480 | tf_op jit(solution)/shard_map/sij,sjr->sir/dot_general | solution.py:135
  299.5 1.9 copy.97
  303.5 2.3 collective-permute-start.12
  310.7 5.2 collective-permute-start.16
  315.9 5.3 collective-permute-start.17
  322.5 38.6 %psum.111 = f32[3,128]{1,0:T(4,128)S(1)} all-reduce(f32[3,128]{1,0:T(4,128)S(1)} %pad_maximum_fusion.15), channel_id=1, replica_groups=mesh['gx'=2,'gy'=4,'gz'=4] {'gx','gy','gz'}, use_global_device_ids=true, to_apply=%region_21.23 | all-reduce | flops 384 | bytes 3072 | tf_op jit(solution)/shard_map/psum | solution.py:209
  361.1 2.9 subtract_reduce_fusion.1
  364.2 75.3 %psum.112 = f32[4,4,4,128]{3,2,1,0:T(4,128)S(1)} all-reduce(f32[4,4,4,128]{3,2,1,0:T(4,128)S(1)} %dynamic_update_slice.17), channel_id=1, replica_groups=mesh['gx'=2,'gy'=4,'gz'=4] {'gy','gz'}, use_global_device_ids=true, to_apply=%region_23.25 | all-reduce | flops 8192 | bytes 65536 | tf_op jit(solution)/shard_map/psum | solution.py:189
  439.5 3.4 psum.113
  446.2 8.0 %fusion.19 = f32[2,1536,128]{1,2,0:T(8,128)} fusion(bf16[2,1536,128]{2,1,0:T(8,128)(2,1)S(1)} %bitcast.461, bf16[2,1,1,1536,1536]{4,3,2,1,0:T(8,128)(2,1)} %param.7), kind=kOutput, calls=%fused_computation.13 | convolution fusion | flops 1207959552 | bytes 11796480 | tf_op jit(solution)/shard_map/sij,sjr->sir/dot_general | solution.py:135
  454.2 3.0 copy.109
  459.0 2.2 collective-permute-start.18
  466.7 5.3 collective-permute-start.22
  471.9 5.2 collective-permute-start.23
  478.8 37.8 %psum.114 = f32[3,128]{1,0:T(4,128)S(1)} all-reduce(f32[3,128]{1,0:T(4,128)S(1)} %pad_maximum_fusion.16), channel_id=1, replica_groups=mesh['gx'=2,'gy'=4,'gz'=4] {'gx','gy','gz'}, use_global_device_ids=true, to_apply=%region_30.32 | all-reduce | flops 384 | bytes 3072 | tf_op jit(solution)/shard_map/psum | solution.py:209
  516.6 3.2 subtract_reduce_fusion
  520.0 75.6 %psum.115 = f32[4,4,4,128]{3,2,1,0:T(4,128)S(1)} all-reduce(f32[4,4,4,128]{3,2,1,0:T(4,128)S(1)} %dynamic_update_slice.18), channel_id=1, replica_groups=mesh['gx'=2,'gy'=4,'gz'=4] {'gy','gz'}, use_global_device_ids=true, to_apply=%region_32.34 | all-reduce | flops 8192 | bytes 65536 | tf_op jit(solution)/shard_map/psum | solution.py:189
  595.6 3.4 psum.116
  601.5 8.1 %fusion.22 = f32[2,1536,128]{1,2,0:T(8,128)} fusion(bf16[2,1536,128]{2,1,0:T(8,128)(2,1)S(1)} %bitcast.459, bf16[2,1,1,1536,1536]{4,3,2,1,0:T(8,128)(2,1)} %param.7), kind=kOutput, calls=%fused_computation.14 | convolution fusion | flops 1207959552 | bytes 11796480 | tf_op jit(solution)/shard_map/sij,sjr->sir/dot_general | solution.py:135
  609.5 3.0 copy.122
  614.3 2.3 collective-permute-start.24
  622.0 5.3 collective-permute-start.28
  627.2 5.2 collective-permute-start.29
  634.1 37.5 %psum.117 = f32[3,128]{1,0:T(4,128)S(1)} all-reduce(f32[3,128]{1,0:T(4,128)S(1)} %pad_maximum_fusion.17), channel_id=1, replica_groups=mesh['gx'=2,'gy'=4,'gz'=4] {'gx','gy','gz'}, use_global_device_ids=true, to_apply=%region_39.41 | all-reduce | flops 384 | bytes 3072 | tf_op jit(solution)/shard_map/psum | solution.py:209
  671.7 2.1 fusion.31
  673.9 75.6 %psum.118 = f32[4,4,4,128]{3,2,1,0:T(4,128)S(1)} all-reduce(f32[4,4,4,128]{3,2,1,0:T(4,128)S(1)} %dynamic_update_slice.19), channel_id=1, replica_groups=mesh['gx'=2,'gy'=4,'gz'=4] {'gy','gz'}, use_global_device_ids=true, to_apply=%region_41.43 | all-reduce | flops 8192 | bytes 65536 | tf_op jit(solution)/shard_map/psum | solution.py:189
  749.5 3.4 psum.119
  753.5 3.0 subtract_bitcast_fusion
  (299 shorter events, 61.9 us)
Async XLA Ops:
  25.4 1.1 copy-start.13
  26.7 0.9 copy-start.5
  28.4 14.6 %collective-permute-start = (f32[1,1,1,256,128]{4,3,0,2,1:T(8,128)}, f32[1,1,1,256,128]{4,3,0,2,1:T(8,128)}, u32[]{:S(2)}, u32[]{:S(2)}) collective-permute-start(f32[1,1,1,256,128]{4,3,0,2,1:T(8,128)} %get-tuple-element.151), channel_id=1, source_target_pairs={{0,16},{1,17},{2,18},{3,19},{4,20},{5,21},{6,22},{7,23},{8,24},{9,... | collective-permute-start | bytes 393224 | tf_op jit(solution)/shard_map/ppermute | solution.py:18
  31.4 16.2 %collective-permute-start.1 = (f32[1,1,1,256,128]{4,3,0,2,1:T(8,128)}, f32[1,1,1,256,128]{4,3,0,2,1:T(8,128)}, u32[]{:S(2)}, u32[]{:S(2)}) collective-permute-start(f32[1,1,1,256,128]{4,3,0,2,1:T(8,128)} %get-tuple-element.152), channel_id=1, source_target_pairs={{16,0},{17,1},{18,2},{19,3},{20,4},{21,5},{22,6},{23,7},{24,8},{25... | collective-permute-start | bytes 393224 | tf_op jit(solution)/shard_map/ppermute | solution.py:20
  33.6 15.1 %collective-permute-start.2 = (f32[2,1,1,256,128]{4,3,0,2,1:T(8,128)}, f32[2,1,1,256,128]{4,3,0,2,1:T(8,128)S(1)}, u32[]{:S(2)}, u32[]{:S(2)}) collective-permute-start(f32[2,1,1,256,128]{4,3,0,2,1:T(8,128)} %get-tuple-element.148), channel_id=1, source_target_pairs={{4,0},{8,4},{12,8},{5,1},{9,5},{13,9},{6,2},{10,6},{14,10},{7,3},{... | collective-permute-start | bytes 786440 | tf_op jit(solution)/shard_map/ppermute | solution.py:20
  34.9 13.8 %collective-permute-start.4 = (f32[2,1,1,256,128]{4,3,0,2,1:T(8,128)}, f32[2,1,1,256,128]{4,3,0,2,1:T(8,128)}, u32[]{:S(2)}, u32[]{:S(2)}) collective-permute-start(f32[2,1,1,256,128]{4,3,0,2,1:T(8,128)} %get-tuple-element.147), channel_id=1, source_target_pairs={{0,4},{4,8},{8,12},{1,5},{5,9},{9,13},{2,6},{6,10},{10,14},{3,7},{... | collective-permute-start | bytes 786440 | tf_op jit(solution)/shard_map/ppermute | solution.py:18
  41.3 10.8 %collective-permute-start.3 = (f32[2,1,1,256,128]{4,3,0,2,1:T(8,128)}, f32[2,1,1,256,128]{4,3,0,2,1:T(8,128)S(1)}, u32[]{:S(2)}, u32[]{:S(2)}) collective-permute-start(f32[2,1,1,256,128]{4,3,0,2,1:T(8,128)} %get-tuple-element.150), channel_id=1, source_target_pairs={{1,0},{2,1},{3,2},{5,4},{6,5},{7,6},{9,8},{10,9},{11,10},{13,12},{... | collective-permute-start | bytes 786440 | tf_op jit(solution)/shard_map/ppermute | solution.py:20
  43.0 11.4 %collective-permute-start.5 = (f32[2,1,1,256,128]{4,3,0,2,1:T(8,128)}, f32[2,1,1,256,128]{4,3,0,2,1:T(8,128)S(1)}, u32[]{:S(2)}, u32[]{:S(2)}) collective-permute-start(f32[2,1,1,256,128]{4,3,0,2,1:T(8,128)} %get-tuple-element.149), channel_id=1, source_target_pairs={{0,1},{1,2},{2,3},{4,5},{5,6},{6,7},{8,9},{9,10},{10,11},{12,13},{... | collective-permute-start | bytes 786440 | tf_op jit(solution)/shard_map/ppermute | solution.py:18
  52.1 2.2 copy-start.14
  147.2 13.5 %collective-permute-start.6 = (f32[1,1,1,256,128]{4,3,0,2,1:T(8,128)S(1)}, f32[1,1,1,256,128]{4,3,0,2,1:T(8,128)S(1)}, u32[]{:S(2)}, u32[]{:S(2)}) collective-permute-start(f32[1,1,1,256,128]{4,3,0,2,1:T(8,128)S(1)} %get-tuple-element.145), channel_id=1, source_target_pairs={{0,16},{1,17},{2,18},{3,19},{4,20},{5,21},{6,22},{7,23},{8,24},{9,... | collective-permute-start | bytes 393224 | tf_op jit(solution)/shard_map/ppermute | solution.py:18
  149.5 16.5 %collective-permute-start.7 = (f32[1,1,1,256,128]{4,3,0,2,1:T(8,128)S(1)}, f32[1,1,1,256,128]{4,3,0,2,1:T(8,128)S(1)}, u32[]{:S(2)}, u32[]{:S(2)}) collective-permute-start(f32[1,1,1,256,128]{4,3,0,2,1:T(8,128)S(1)} %get-tuple-element.146), channel_id=1, source_target_pairs={{16,0},{17,1},{18,2},{19,3},{20,4},{21,5},{22,6},{23,7},{24,8},{25... | collective-permute-start | bytes 393224 | tf_op jit(solution)/shard_map/ppermute | solution.py:20
  151.6 14.6 %collective-permute-start.8 = (f32[2,1,1,256,128]{4,3,0,2,1:T(8,128)S(1)}, f32[2,1,1,256,128]{4,3,0,2,1:T(8,128)S(1)}, u32[]{:S(2)}, u32[]{:S(2)}) collective-permute-start(f32[2,1,1,256,128]{4,3,0,2,1:T(8,128)S(1)} %get-tuple-element.142), channel_id=1, source_target_pairs={{4,0},{8,4},{12,8},{5,1},{9,5},{13,9},{6,2},{10,6},{14,10},{7,3},{... | collective-permute-start | bytes 786440 | tf_op jit(solution)/shard_map/ppermute | solution.py:20
  153.6 12.5 %collective-permute-start.9 = (f32[2,1,1,256,128]{4,3,0,2,1:T(8,128)S(1)}, f32[2,1,1,256,128]{4,3,0,2,1:T(8,128)S(1)}, u32[]{:S(2)}, u32[]{:S(2)}) collective-permute-start(f32[2,1,1,256,128]{4,3,0,2,1:T(8,128)S(1)} %get-tuple-element.144), channel_id=1, source_target_pairs={{1,0},{2,1},{3,2},{5,4},{6,5},{7,6},{9,8},{10,9},{11,10},{13,12},{... | collective-permute-start | bytes 786440 | tf_op jit(solution)/shard_map/ppermute | solution.py:20
  154.9 51.6 %collective-permute-start.10 = (f32[2,1,1,256,128]{4,3,0,2,1:T(8,128)}, f32[2,1,1,256,128]{4,3,0,2,1:T(8,128)}, u32[]{:S(2)}, u32[]{:S(2)}) collective-permute-start(f32[2,1,1,256,128]{4,3,0,2,1:T(8,128)} %get-tuple-element.141), channel_id=1, source_target_pairs={{0,4},{4,8},{8,12},{1,5},{5,9},{9,13},{2,6},{6,10},{10,14},{3,7},{... | collective-permute-start | bytes 786440 | tf_op jit(solution)/shard_map/ppermute | solution.py:18
  160.7 45.8 %collective-permute-start.11 = (f32[2,1,1,256,128]{4,3,2,0,1:T(8,128)}, f32[2,1,1,256,128]{4,3,2,0,1:T(8,128)}, u32[]{:S(2)}, u32[]{:S(2)}) collective-permute-start(f32[2,1,1,256,128]{4,3,2,0,1:T(8,128)} %get-tuple-element.143), channel_id=1, source_target_pairs={{0,1},{1,2},{2,3},{4,5},{5,6},{6,7},{8,9},{9,10},{10,11},{12,13},{... | collective-permute-start | bytes 786440 | tf_op jit(solution)/shard_map/ppermute | solution.py:18
  166.1 40.4 %copy-start.19 = (f32[128]{0:T(128)S(1)}, f32[128]{0:T(128)}, u32[]{:S(2)}) copy-start(f32[128]{0:T(128)} %get-tuple-element.208) | copy-start | bytes 1540
  166.1 40.4 %copy-start.20 = (f32[128]{0:T(128)S(1)}, f32[128]{0:T(128)}, u32[]{:S(2)}) copy-start(f32[128]{0:T(128)} %multiply_reduce_fusion.20) | copy-start | bytes 1540
  206.5 82.3 %copy-start.15 = (f32[128]{0:T(128)}, f32[128]{0:T(128)S(1)}, u32[]{:S(2)}) copy-start(f32[128]{0:T(128)S(1)} %bitcast_divide_fusion.3) | copy-start | bytes 1540
  290.6 0.9 copy-start.8
  290.6 153.1 %copy-start.1 = (f32[2,1,1,3,256,128]{5,4,3,0,2,1:T(8,128)}, f32[2,1,1,3,256,128]{5,4,3,0,2,1:T(8,128)S(1)}, u32[]{:S(2)}) copy-start(f32[2,1,1,3,256,128]{5,4,3,0,2,1:T(8,128)S(1)} %get-tuple-element.49) | copy-start | bytes 2359300
  301.4 1.2 copy-start.3
  302.5 0.9 copy-start.7
  303.5 12.4 %collective-permute-start.12 = (f32[1,1,1,256,128]{4,3,0,2,1:T(8,128)S(1)}, f32[1,1,1,256,128]{4,3,0,2,1:T(8,128)S(1)}, u32[]{:S(2)}, u32[]{:S(2)}) collective-permute-start(f32[1,1,1,256,128]{4,3,0,2,1:T(8,128)S(1)} %get-tuple-element.139), channel_id=1, source_target_pairs={{0,16},{1,17},{2,18},{3,19},{4,20},{5,21},{6,22},{7,23},{8,24},{9,... | collective-permute-start | bytes 393224 | tf_op jit(solution)/shard_map/ppermute | solution.py:18
  305.8 15.4 %collective-permute-start.13 = (f32[1,1,1,256,128]{4,3,0,2,1:T(8,128)S(1)}, f32[1,1,1,256,128]{4,3,0,2,1:T(8,128)S(1)}, u32[]{:S(2)}, u32[]{:S(2)}) collective-permute-start(f32[1,1,1,256,128]{4,3,0,2,1:T(8,128)S(1)} %get-tuple-element.140), channel_id=1, source_target_pairs={{16,0},{17,1},{18,2},{19,3},{20,4},{21,5},{22,6},{23,7},{24,8},{25... | collective-permute-start | bytes 393224 | tf_op jit(solution)/shard_map/ppermute | solution.py:20
  307.9 13.4 %collective-permute-start.14 = (f32[2,1,1,256,128]{4,3,0,1,2:T(8,128)S(1)}, f32[2,1,1,256,128]{4,3,0,1,2:T(8,128)S(1)}, u32[]{:S(2)}, u32[]{:S(2)}) collective-permute-start(f32[2,1,1,256,128]{4,3,0,1,2:T(8,128)S(1)} %get-tuple-element.135), channel_id=1, source_target_pairs={{4,0},{8,4},{12,8},{5,1},{9,5},{13,9},{6,2},{10,6},{14,10},{7,3},{... | collective-permute-start | bytes 786440 | tf_op jit(solution)/shard_map/ppermute | solution.py:20
  309.2 12.1 %copy-start.2 = (f32[2,1,1,3,256,128]{5,4,3,0,2,1:T(8,128)S(1)}, f32[2,1,1,3,256,128]{5,4,3,0,2,1:T(8,128)}, u32[]{:S(2)}) copy-start(f32[2,1,1,3,256,128]{5,4,3,0,2,1:T(8,128)} %get-tuple-element.57) | copy-start | bytes 2359300
  309.3 12.1 %copy-start.4 = (f32[2,1536,128]{2,1,0:T(8,128)S(1)}, f32[2,1536,128]{2,1,0:T(8,128)}, u32[]{:S(2)}) copy-start(f32[2,1536,128]{2,1,0:T(8,128)} %copy-done.3) | copy-start | bytes 4718596
  309.3 12.0 %collective-permute-start.15 = (f32[2,1,1,256,128]{4,3,0,2,1:T(8,128)S(1)}, f32[2,1,1,256,128]{4,3,0,2,1:T(8,128)S(1)}, u32[]{:S(2)}, u32[]{:S(2)}) collective-permute-start(f32[2,1,1,256,128]{4,3,0,2,1:T(8,128)S(1)} %get-tuple-element.137), channel_id=1, source_target_pairs={{1,0},{2,1},{3,2},{5,4},{6,5},{7,6},{9,8},{10,9},{11,10},{13,12},{... | collective-permute-start | bytes 786440 | tf_op jit(solution)/shard_map/ppermute | solution.py:20
  310.7 50.4 %collective-permute-start.16 = (f32[2,1,1,256,128]{4,3,0,1,2:T(8,128)}, f32[2,1,1,256,128]{4,3,0,1,2:T(8,128)}, u32[]{:S(2)}, u32[]{:S(2)}) collective-permute-start(f32[2,1,1,256,128]{4,3,0,1,2:T(8,128)} %get-tuple-element.136), channel_id=1, source_target_pairs={{0,4},{4,8},{8,12},{1,5},{5,9},{9,13},{2,6},{6,10},{10,14},{3,7},{... | collective-permute-start | bytes 786440 | tf_op jit(solution)/shard_map/ppermute | solution.py:18
  315.9 45.2 %collective-permute-start.17 = (f32[2,1,1,256,128]{4,3,0,2,1:T(8,128)S(1)}, f32[2,1,1,256,128]{4,3,0,2,1:T(8,128)}, u32[]{:S(2)}, u32[]{:S(2)}) collective-permute-start(f32[2,1,1,256,128]{4,3,0,2,1:T(8,128)S(1)} %get-tuple-element.138), channel_id=1, source_target_pairs={{0,1},{1,2},{2,3},{4,5},{5,6},{6,7},{8,9},{9,10},{10,11},{12,13},{... | collective-permute-start | bytes 786440 | tf_op jit(solution)/shard_map/ppermute | solution.py:18
  361.1 82.5 %copy-start.21 = (f32[128]{0:T(128)}, f32[128]{0:T(128)S(1)}, u32[]{:S(2)}) copy-start(f32[128]{0:T(128)S(1)} %bitcast_divide_fusion.2) | copy-start | bytes 1540
  364.1 113.9 %copy-start = (f32[2,1,1,3,256,128]{5,4,3,0,2,1:T(8,128)}, f32[2,1,1,3,256,128]{5,4,3,0,2,1:T(8,128)S(1)}, u32[]{:S(2)}) copy-start(f32[2,1,1,3,256,128]{5,4,3,0,2,1:T(8,128)S(1)} %get-tuple-element.46) | copy-start | bytes 2359300
  459.0 13.0 %collective-permute-start.18 = (f32[1,1,1,256,128]{4,3,0,2,1:T(8,128)S(1)}, f32[1,1,1,256,128]{4,3,0,2,1:T(8,128)S(1)}, u32[]{:S(2)}, u32[]{:S(2)}) collective-permute-start(f32[1,1,1,256,128]{4,3,0,2,1:T(8,128)S(1)} %get-tuple-element.133), channel_id=1, source_target_pairs={{0,16},{1,17},{2,18},{3,19},{4,20},{5,21},{6,22},{7,23},{8,24},{9,... | collective-permute-start | bytes 393224 | tf_op jit(solution)/shard_map/ppermute | solution.py:18
  461.2 16.0 %collective-permute-start.19 = (f32[1,1,1,256,128]{4,3,0,2,1:T(8,128)S(1)}, f32[1,1,1,256,128]{4,3,0,2,1:T(8,128)S(1)}, u32[]{:S(2)}, u32[]{:S(2)}) collective-permute-start(f32[1,1,1,256,128]{4,3,0,2,1:T(8,128)S(1)} %get-tuple-element.134), channel_id=1, source_target_pairs={{16,0},{17,1},{18,2},{19,3},{20,4},{21,5},{22,6},{23,7},{24,8},{25... | collective-permute-start | bytes 393224 | tf_op jit(solution)/shard_map/ppermute | solution.py:20
  463.3 14.7 %collective-permute-start.20 = (f32[2,1,1,256,128]{4,3,0,2,1:T(8,128)S(1)}, f32[2,1,1,256,128]{4,3,0,2,1:T(8,128)S(1)}, u32[]{:S(2)}, u32[]{:S(2)}) collective-permute-start(f32[2,1,1,256,128]{4,3,0,2,1:T(8,128)S(1)} %get-tuple-element.129), channel_id=1, source_target_pairs={{4,0},{8,4},{12,8},{5,1},{9,5},{13,9},{6,2},{10,6},{14,10},{7,3},{... | collective-permute-start | bytes 786440 | tf_op jit(solution)/shard_map/ppermute | solution.py:20
  465.4 12.6 %collective-permute-start.21 = (f32[2,1,1,256,128]{4,3,0,2,1:T(8,128)S(1)}, f32[2,1,1,256,128]{4,3,0,2,1:T(8,128)S(1)}, u32[]{:S(2)}, u32[]{:S(2)}) collective-permute-start(f32[2,1,1,256,128]{4,3,0,2,1:T(8,128)S(1)} %get-tuple-element.131), channel_id=1, source_target_pairs={{1,0},{2,1},{3,2},{5,4},{6,5},{7,6},{9,8},{10,9},{11,10},{13,12},{... | collective-permute-start | bytes 786440 | tf_op jit(solution)/shard_map/ppermute | solution.py:20
  466.7 50.0 %collective-permute-start.22 = (f32[2,1,1,256,128]{4,3,0,2,1:T(8,128)}, f32[2,1,1,256,128]{4,3,0,2,1:T(8,128)}, u32[]{:S(2)}, u32[]{:S(2)}) collective-permute-start(f32[2,1,1,256,128]{4,3,0,2,1:T(8,128)} %get-tuple-element.130), channel_id=1, source_target_pairs={{0,4},{4,8},{8,12},{1,5},{5,9},{9,13},{2,6},{6,10},{10,14},{3,7},{... | collective-permute-start | bytes 786440 | tf_op jit(solution)/shard_map/ppermute | solution.py:18
  471.9 44.7 %collective-permute-start.23 = (f32[2,1,1,256,128]{4,3,2,0,1:T(8,128)}, f32[2,1,1,256,128]{4,3,2,0,1:T(8,128)}, u32[]{:S(2)}, u32[]{:S(2)}) collective-permute-start(f32[2,1,1,256,128]{4,3,2,0,1:T(8,128)} %get-tuple-element.132), channel_id=1, source_target_pairs={{0,1},{1,2},{2,3},{4,5},{5,6},{6,7},{8,9},{9,10},{10,11},{12,13},{... | collective-permute-start | bytes 786440 | tf_op jit(solution)/shard_map/ppermute | solution.py:18
  516.6 83.0 %copy-start.17 = (f32[128]{0:T(128)}, f32[128]{0:T(128)S(1)}, u32[]{:S(2)}) copy-start(f32[128]{0:T(128)S(1)} %bitcast_divide_fusion.1) | copy-start | bytes 1540
  614.3 13.0 %collective-permute-start.24 = (f32[1,1,1,256,128]{4,3,0,2,1:T(8,128)S(1)}, f32[1,1,1,256,128]{4,3,0,2,1:T(8,128)S(1)}, u32[]{:S(2)}, u32[]{:S(2)}) collective-permute-start(f32[1,1,1,256,128]{4,3,0,2,1:T(8,128)S(1)} %get-tuple-element.127), channel_id=1, source_target_pairs={{0,16},{1,17},{2,18},{3,19},{4,20},{5,21},{6,22},{7,23},{8,24},{9,... | collective-permute-start | bytes 393224 | tf_op jit(solution)/shard_map/ppermute | solution.py:18
  616.5 16.0 %collective-permute-start.25 = (f32[1,1,1,256,128]{4,3,0,2,1:T(8,128)S(1)}, f32[1,1,1,256,128]{4,3,0,2,1:T(8,128)S(1)}, u32[]{:S(2)}, u32[]{:S(2)}) collective-permute-start(f32[1,1,1,256,128]{4,3,0,2,1:T(8,128)S(1)} %get-tuple-element.128), channel_id=1, source_target_pairs={{16,0},{17,1},{18,2},{19,3},{20,4},{21,5},{22,6},{23,7},{24,8},{25... | collective-permute-start | bytes 393224 | tf_op jit(solution)/shard_map/ppermute | solution.py:20
  618.6 14.7 %collective-permute-start.26 = (f32[2,1,1,256,128]{4,3,0,2,1:T(8,128)S(1)}, f32[2,1,1,256,128]{4,3,0,2,1:T(8,128)S(1)}, u32[]{:S(2)}, u32[]{:S(2)}) collective-permute-start(f32[2,1,1,256,128]{4,3,0,2,1:T(8,128)S(1)} %get-tuple-element.124), channel_id=1, source_target_pairs={{4,0},{8,4},{12,8},{5,1},{9,5},{13,9},{6,2},{10,6},{14,10},{7,3},{... | collective-permute-start | bytes 786440 | tf_op jit(solution)/shard_map/ppermute | solution.py:20
  620.7 12.6 %collective-permute-start.27 = (f32[2,1,1,256,128]{4,3,0,2,1:T(8,128)S(1)}, f32[2,1,1,256,128]{4,3,0,2,1:T(8,128)S(1)}, u32[]{:S(2)}, u32[]{:S(2)}) collective-permute-start(f32[2,1,1,256,128]{4,3,0,2,1:T(8,128)S(1)} %get-tuple-element.126), channel_id=1, source_target_pairs={{1,0},{2,1},{3,2},{5,4},{6,5},{7,6},{9,8},{10,9},{11,10},{13,12},{... | collective-permute-start | bytes 786440 | tf_op jit(solution)/shard_map/ppermute | solution.py:20
  622.0 49.7 %collective-permute-start.28 = (f32[2,1,1,256,128]{4,3,0,2,1:T(8,128)}, f32[2,1,1,256,128]{4,3,0,2,1:T(8,128)}, u32[]{:S(2)}, u32[]{:S(2)}) collective-permute-start(f32[2,1,1,256,128]{4,3,0,2,1:T(8,128)} %get-tuple-element.123), channel_id=1, source_target_pairs={{0,4},{4,8},{8,12},{1,5},{5,9},{9,13},{2,6},{6,10},{10,14},{3,7},{... | collective-permute-start | bytes 786440 | tf_op jit(solution)/shard_map/ppermute | solution.py:18
  627.2 44.4 %collective-permute-start.29 = (f32[2,1,1,256,128]{4,3,2,0,1:T(8,128)}, f32[2,1,1,256,128]{4,3,2,0,1:T(8,128)}, u32[]{:S(2)}, u32[]{:S(2)}) collective-permute-start(f32[2,1,1,256,128]{4,3,2,0,1:T(8,128)} %get-tuple-element.125), channel_id=1, source_target_pairs={{0,1},{1,2},{2,3},{4,5},{5,6},{6,7},{8,9},{9,10},{10,11},{12,13},{... | collective-permute-start | bytes 786440 | tf_op jit(solution)/shard_map/ppermute | solution.py:18
  671.7 2.1 copy-start.22
  671.7 81.8 %copy-start.16 = (f32[128]{0:T(128)S(1)}, f32[128]{0:T(128)}, u32[]{:S(2)}) copy-start(f32[128]{0:T(128)} %copy-done.15) | copy-start | bytes 1540
  671.7 81.8 %copy-start.18 = (f32[128]{0:T(128)S(1)}, f32[128]{0:T(128)}, u32[]{:S(2)}) copy-start(f32[128]{0:T(128)} %copy-done.17) | copy-start | bytes 1540
  (5 other events, 3.9 us)
